TPU v7x, 32 devices: a whole 2x2x4 slice. The times are simulated.
32 devices in a mesh: dp: 8 (over z, y), tensor: 4 (over x, core).
Axes of the slice: x: 2, y: 2, z: 4, core: 2. Of those that a mesh axis runs over, the one named last changes fastest.
Arguments:
- tokens: bfloat16 [12288, 768], P('dp'), may hold values from -6 to 6
- segment_ids: int32 [24, 512], P('dp'), may hold values from 0 to 16, as said below
- prev_scores: bfloat16 [24, 12, 512, 512], P('dp', 'tensor'), may hold values from -6 to 6
- out_grad: bfloat16 [12288, 768], P('dp'), may hold values from -6 to 6
- attn_in_master: float32 [3, 768, 768], P(None, 'dp', 'tensor'), may hold values from -0.21875 to 0.21875
- attn_out_master: float32 [768, 768], P('tensor', 'dp'), may hold values from -0.875 to 0.875
- ffn_in_master: float32 [768, 3072], P('dp', 'tensor'), may hold values from -0.21875 to 0.21875
- ffn_out_master: float32 [3072, 768], P('tensor', 'dp'), may hold values from -0.109375 to 0.109375
- attn_in_first: float32 [3, 768, 768], P(None, 'dp', 'tensor'), may hold values from -0.0024414062 to 0.0024414062
- attn_out_first: float32 [768, 768], P('tensor', 'dp'), may hold values from -0.0024414062 to 0.0024414062
- ffn_in_first: float32 [768, 3072], P('dp', 'tensor'), may hold values from -0.0024414062 to 0.0024414062
- ffn_out_first: float32 [3072, 768], P('tensor', 'dp'), may hold values from -0.0024414062 to 0.0024414062
- attn_in_second: float32 [3, 768, 768], P(None, 'dp', 'tensor'), may hold values from 1.4110135e-07 to 5.644054e-07
- attn_out_second: float32 [768, 768], P('tensor', 'dp'), may hold values from 1.4110135e-07 to 5.644054e-07
- ffn_in_second: float32 [768, 3072], P('dp', 'tensor'), may hold values from 1.4110135e-07 to 5.644054e-07
- ffn_out_second: float32 [3072, 768], P('tensor', 'dp'), may hold values from 1.4110135e-07 to 5.644054e-07
- qv_bias: float32 [2, 768], P(None, 'tensor'), may hold values from -1.75 to 1.75
- ffn_bias: float32 [3072], P('tensor'), may hold values from -1.75 to 1.75
- row_params: float32 [6, 768], replicated, may hold values from -0.75 to 1.65, as said below
- qv_bias_first: float32 [2, 768], P(None, 'tensor'), may hold values from -0.009765625 to 0.009765625
- ffn_bias_first: float32 [3072], P('tensor'), may hold values from -0.0024414062 to 0.0024414062
- row_params_first: float32 [6, 768], replicated, may hold values from -0.009765625 to 0.009765625
- qv_bias_second: float32 [2, 768], P(None, 'tensor'), may hold values from 2.2576216e-06 to 9.030487e-06
- ffn_bias_second: float32 [3072], P('tensor'), may hold values from 7.0550676e-08 to 2.822027e-07
- row_params_second: float32 [6, 768], replicated, may hold values from 2.2576216e-06 to 9.030487e-06
Outputs:
- out_tokens: bfloat16 [12288, 768], P('dp')
- tokens_grad: float32 [12288, 768], P('dp')
- scores_grad: float32 [24, 12, 512, 512], P('dp', 'tensor')
- grad_norm: float32 [], replicated
- attn_in_new: float32 [3, 768, 768], P(None, 'dp', 'tensor')
- attn_out_new: float32 [768, 768], P('tensor', 'dp')
- ffn_in_new: float32 [768, 3072], P('dp', 'tensor')
- ffn_out_new: float32 [3072, 768], P('tensor', 'dp')
- attn_in_first_new: float32 [3, 768, 768], P(None, 'dp', 'tensor')
- attn_out_first_new: float32 [768, 768], P('tensor', 'dp')
- ffn_in_first_new: float32 [768, 3072], P('dp', 'tensor')
- ffn_out_first_new: float32 [3072, 768], P('tensor', 'dp')
- attn_in_second_new: float32 [3, 768, 768], P(None, 'dp', 'tensor')
- attn_out_second_new: float32 [768, 768], P('tensor', 'dp')
- ffn_in_second_new: float32 [768, 3072], P('dp', 'tensor')
- ffn_out_second_new: float32 [3072, 768], P('tensor', 'dp')
- attn_in_copy: bfloat16 [3, 768, 768], P(None, 'dp', 'tensor')
- attn_out_copy: bfloat16 [768, 768], P('tensor', 'dp')
- ffn_in_copy: bfloat16 [768, 3072], P('dp', 'tensor')
- ffn_out_copy: bfloat16 [3072, 768], P('tensor', 'dp')
- qv_bias_new: float32 [2, 768], P(None, 'tensor')
- ffn_bias_new: float32 [3072], P('tensor')
- row_params_new: float32 [6, 768], replicated
- qv_bias_first_new: float32 [2, 768], P(None, 'tensor')
- ffn_bias_first_new: float32 [3072], P('tensor')
- row_params_first_new: float32 [6, 768], replicated
- qv_bias_second_new: float32 [2, 768], P(None, 'tensor')
- ffn_bias_second_new: float32 [3072], P('tensor')
- row_params_second_new: float32 [6, 768], replicated
Inputs may be any that keep to these rules, and one draw needn't show every extreme that they name: `segment_ids`: in each pack, live slots come first and empty slots (0) last; live ids start at 1 and rise by one from one sequence to the next; sequences start at multiples of 32 slots; a pack holds 128, 256, 384 or 512 live slots; the first pack holds one sequence of 512 slots, the second pack 3 * 128 live slots, the last pack 16 sequences of 32 slots. `row_params`: rows 0 and 1 lie between 0.35 and 1.65.
All inputs are finite; a program needn't handle non-finite values.
Results may differ from a plain program's by a relative error of at most 0.012.
The roundings to bfloat16 on the way count: a program that leaves them out, or rounds other values in their place, can miss the bound.
Values may be sent and summed in bfloat16 or wider, within the bound.
A program may use at most 128 MiB of HBM per device.

v0:
```python
from functools import partial
import jax
import jax.numpy as jnp
from jax import lax
from jax.sharding import PartitionSpec as P

D = 768
STEP = 5
beta_one = 0.5
beta_two = 0.5
weight_decay = 0.01
adam_eps = 1e-08
norm_eps = 1e-06
small_rate = 0.5


def layer_norm(rows_in, gain_row, shift_row):
    row_mean = jnp.mean(rows_in, axis=-1, keepdims=True)
    centred = rows_in - row_mean
    spread = jnp.mean(centred * centred, axis=-1, keepdims=True)
    return centred * lax.rsqrt(spread + norm_eps) * gain_row + shift_row


def masked_scores(scale, query_heads, key_heads, prev_block, seg_ids):
    same_seq = seg_ids[:, None] == seg_ids[None, :]
    scores = jnp.einsum(
        "qhe,khe->hqk", query_heads, key_heads, preferred_element_type=jnp.float32
    ) * scale + prev_block.astype(jnp.float32)
    return jnp.where(same_seq[None], scores, -1000000000.0)


def attend(scale, pieces):
    query_heads, key_heads, value_heads, prev_block, seg_ids = pieces
    scores = masked_scores(scale, query_heads, key_heads, prev_block, seg_ids)
    row_top = jnp.max(scores, axis=-1, keepdims=True)
    expo = jnp.exp(scores - row_top)
    row_total = jnp.sum(expo, axis=-1, keepdims=True)
    weights_low = (expo / row_total).astype(jnp.bfloat16)
    context_heads = jnp.einsum(
        "hqk,khe->qhe", weights_low, value_heads, preferred_element_type=jnp.float32
    )
    return (context_heads.astype(jnp.bfloat16), row_top + jnp.log(row_total))


def attend_back(scale, pieces):
    query_heads, key_heads, value_heads, prev_block, seg_ids, row_lse, grad_heads = pieces
    scores = masked_scores(scale, query_heads, key_heads, prev_block, seg_ids)
    soft = jnp.exp(scores - row_lse)
    soft_low = soft.astype(jnp.bfloat16)
    grad_soft = jnp.einsum(
        "qhe,khe->hqk", grad_heads, value_heads, preferred_element_type=jnp.float32
    )
    row_dot = jnp.sum(soft * grad_soft, axis=-1, keepdims=True)
    score_grad = (soft * (grad_soft - row_dot)).astype(jnp.bfloat16)
    grad_query = (
        jnp.einsum("hqk,khe->qhe", score_grad, key_heads, preferred_element_type=jnp.float32)
        * scale
    ).astype(jnp.bfloat16)
    grad_key = (
        jnp.einsum("hqk,qhe->khe", score_grad, query_heads, preferred_element_type=jnp.float32)
        * scale
    ).astype(jnp.bfloat16)
    grad_value = jnp.einsum(
        "hqk,qhe->khe", soft_low, grad_heads, preferred_element_type=jnp.float32
    ).astype(jnp.bfloat16)
    return (grad_query, grad_key, grad_value, score_grad.astype(jnp.float32))


def adam_update(weight, gradient, first_moment, second_moment, decay_rate, learn_rate):
    first_new = beta_one * first_moment + (1.0 - beta_one) * gradient
    second_new = beta_two * second_moment + (1.0 - beta_two) * gradient * gradient
    corrected = (
        first_new
        / (1.0 - beta_one**STEP)
        / (jnp.sqrt(second_new / (1.0 - beta_two**STEP)) + adam_eps)
    )
    return (weight - learn_rate * (corrected + decay_rate * weight), first_new, second_new)


def on_device(
    tokens,
    segment_ids,
    prev_scores,
    out_grad,
    attn_in_master,
    attn_out_master,
    ffn_in_master,
    ffn_out_master,
    attn_in_first,
    attn_out_first,
    ffn_in_first,
    ffn_out_first,
    attn_in_second,
    attn_out_second,
    ffn_in_second,
    ffn_out_second,
    qv_bias,
    ffn_bias,
    row_params,
    qv_bias_first,
    ffn_bias_first,
    row_params_first,
    qv_bias_second,
    ffn_bias_second,
    row_params_second,
):
    attn_in, attn_out, ffn_in, ffn_out = (
        lax.all_gather(attn_in_master.astype(jnp.bfloat16), "dp", axis=1, tiled=True),
        lax.all_gather(attn_out_master.astype(jnp.bfloat16), "dp", axis=1, tiled=True),
        lax.all_gather(ffn_in_master.astype(jnp.bfloat16), "dp", axis=0, tiled=True),
        lax.all_gather(ffn_out_master.astype(jnp.bfloat16), "dp", axis=1, tiled=True),
    )
    pack_count, pack_len = segment_ids.shape
    head_count = prev_scores.shape[1]
    head_width = attn_in.shape[2] // head_count
    scale = head_width ** (-0.5)
    token_count = tokens.shape[0]
    dp_count = lax.axis_size("dp")
    tensor_count = lax.axis_size("tensor")

    def split_heads(matrix):
        return matrix.reshape(pack_count, pack_len, head_count, head_width)

    projected = jnp.einsum("td,cde->cte", tokens, attn_in, preferred_element_type=jnp.float32)
    query_rows = (projected[0] + qv_bias[0]).astype(jnp.bfloat16)
    key_rows = projected[1].astype(jnp.bfloat16)
    value_rows = (projected[2] + qv_bias[1]).astype(jnp.bfloat16)
    query_heads = split_heads(query_rows)
    key_heads = split_heads(key_rows)
    value_heads = split_heads(value_rows)
    context_heads, row_lse = lax.map(
        partial(attend, scale), (query_heads, key_heads, value_heads, prev_scores, segment_ids)
    )
    context = context_heads.reshape(token_count, -1)
    attn_partial = jnp.dot(context, attn_out, preferred_element_type=jnp.float32)
    live_whole = (segment_ids > 0).astype(jnp.float32).reshape(token_count, 1)
    rows_start = tokens.astype(jnp.float32)
    attended = lax.psum(attn_partial, "tensor") + row_params[2]
    cotangent = out_grad.astype(jnp.float32)
    residual_one = rows_start + attended
    normed, first_pull = jax.vjp(layer_norm, residual_one, row_params[0], row_params[3])
    normed_low = normed.astype(jnp.bfloat16)
    pre_act = jnp.dot(normed_low, ffn_in, preferred_element_type=jnp.float32) + ffn_bias
    activation, gelu_pull = jax.vjp(partial(jax.nn.gelu, approximate=False), pre_act)
    act_low = activation.astype(jnp.bfloat16)
    ffn_partial = jnp.dot(act_low, ffn_out, preferred_element_type=jnp.float32)
    ffn_output = lax.psum(ffn_partial, "tensor") + row_params[4]

    def final_norm(rows_in, gain_row, shift_row):
        return layer_norm(rows_in, gain_row, shift_row) * live_whole

    final_rows, second_pull = jax.vjp(final_norm, normed + ffn_output, row_params[1], row_params[5])
    final_low = final_rows.astype(jnp.bfloat16)
    grad_res_two, grad_gain_two, grad_shift_two = second_pull(cotangent)
    grad_ffn_low = grad_res_two.astype(jnp.bfloat16)
    grad_ffn_out_bias = jnp.sum(grad_ffn_low.astype(jnp.float32), axis=0)
    grad_ffn_out = jnp.einsum(
        "tf,td->fd", act_low, grad_ffn_low, preferred_element_type=jnp.float32
    )
    grad_act = jnp.einsum("td,fd->tf", grad_ffn_low, ffn_out, preferred_element_type=jnp.float32)
    (grad_pre,) = gelu_pull(grad_act)
    grad_pre_low = grad_pre.astype(jnp.bfloat16)
    grad_ffn_bias = jnp.sum(grad_pre_low.astype(jnp.float32), axis=0)
    grad_ffn_in = jnp.einsum(
        "td,tf->df", normed_low, grad_pre_low, preferred_element_type=jnp.float32
    )
    hidden_part = jnp.einsum("tf,df->td", grad_pre_low, ffn_in, preferred_element_type=jnp.float32)
    grad_normed = grad_res_two + lax.psum(hidden_part, "tensor")
    grad_res_one, grad_gain_one, grad_shift_one = first_pull(grad_normed)
    att_low = grad_res_one.astype(jnp.bfloat16)
    grad_att_bias = jnp.sum(att_low.astype(jnp.float32), axis=0)
    grad_attn_out = jnp.einsum("te,td->ed", context, att_low, preferred_element_type=jnp.float32)
    grad_context = jnp.einsum(
        "td,ed->te", att_low, attn_out, preferred_element_type=jnp.float32
    ).astype(jnp.bfloat16)
    grad_query, grad_key, grad_value, scores_grad = lax.map(
        partial(attend_back, scale),
        (
            query_heads,
            key_heads,
            value_heads,
            prev_scores,
            segment_ids,
            row_lse,
            split_heads(grad_context),
        ),
    )
    grad_proj = jnp.stack(
        [
            grad_query.reshape(token_count, -1),
            grad_key.reshape(token_count, -1),
            grad_value.reshape(token_count, -1),
        ]
    )
    grad_attn_in = jnp.einsum("td,cte->cde", tokens, grad_proj, preferred_element_type=jnp.float32)
    grad_qv_bias = jnp.stack(
        [
            jnp.sum(grad_proj[0].astype(jnp.float32), axis=0),
            jnp.sum(grad_proj[2].astype(jnp.float32), axis=0),
        ]
    )
    input_part = jnp.einsum("cte,cde->td", grad_proj, attn_in, preferred_element_type=jnp.float32)
    norm_stack = jnp.stack([grad_gain_one, grad_gain_two, grad_shift_one, grad_shift_two])
    tokens_grad = grad_res_one + lax.psum(input_part, "tensor")
    grad_rows = jnp.stack(
        [
            norm_stack[0],
            norm_stack[1],
            grad_att_bias,
            norm_stack[2],
            grad_ffn_out_bias,
            norm_stack[3],
        ]
    )
    summed = lax.psum(
        (
            grad_attn_in,
            grad_attn_out,
            grad_ffn_in,
            grad_ffn_out,
            grad_qv_bias,
            grad_ffn_bias,
            grad_rows,
        ),
        "dp",
    )
    dp_index = lax.axis_index("dp")

    def own_part(whole_grad, shard, along):
        extent = shard.shape[along]
        return lax.dynamic_slice_in_dim(whole_grad, dp_index * extent, extent, along)

    shares = (
        own_part(summed[0], attn_in_master, 1),
        own_part(summed[1], attn_out_master, 1),
        own_part(summed[2], ffn_in_master, 0),
        own_part(summed[3], ffn_out_master, 1),
    )
    small_sums = (summed[4], summed[5], summed[6])
    local_squares = jnp.float32(0.0)
    for share in shares:
        local_squares = local_squares + jnp.sum(share * share)
    local_squares = (
        local_squares
        + (jnp.sum(small_sums[0] * small_sums[0]) + jnp.sum(small_sums[1] * small_sums[1]))
        / dp_count
    )
    local_squares = local_squares + jnp.sum(small_sums[2] * small_sums[2]) / (
        dp_count * tensor_count
    )
    total_squares = lax.psum(local_squares, ("dp", "tensor"))
    grad_norm = jnp.sqrt(total_squares)
    factor = 1.0 / jnp.maximum(grad_norm, 1.0)
    olds = (
        attn_in_master,
        attn_out_master,
        ffn_in_master,
        ffn_out_master,
        qv_bias,
        ffn_bias,
        row_params,
    )
    firsts = (
        attn_in_first,
        attn_out_first,
        ffn_in_first,
        ffn_out_first,
        qv_bias_first,
        ffn_bias_first,
        row_params_first,
    )
    seconds = (
        attn_in_second,
        attn_out_second,
        ffn_in_second,
        ffn_out_second,
        qv_bias_second,
        ffn_bias_second,
        row_params_second,
    )
    gradients = (
        shares[0],
        shares[1],
        shares[2],
        shares[3],
        small_sums[0],
        small_sums[1],
        small_sums[2],
    )
    decays = (weight_decay, weight_decay, weight_decay, weight_decay, 0.0, 0.0, 0.0)
    big_rate = D ** (-0.5)
    rates = (big_rate, big_rate, big_rate, big_rate, small_rate, small_rate, small_rate)
    updated = [
        adam_update(
            olds[place],
            gradients[place] * factor,
            firsts[place],
            seconds[place],
            decays[place],
            rates[place],
        )
        for place in range(7)
    ]
    return (
        final_low,
        tokens_grad,
        scores_grad,
        grad_norm,
        updated[0][0],
        updated[1][0],
        updated[2][0],
        updated[3][0],
        updated[0][1],
        updated[1][1],
        updated[2][1],
        updated[3][1],
        updated[0][2],
        updated[1][2],
        updated[2][2],
        updated[3][2],
        updated[0][0].astype(jnp.bfloat16),
        updated[1][0].astype(jnp.bfloat16),
        updated[2][0].astype(jnp.bfloat16),
        updated[3][0].astype(jnp.bfloat16),
        updated[4][0],
        updated[5][0],
        updated[6][0],
        updated[4][1],
        updated[5][1],
        updated[6][1],
        updated[4][2],
        updated[5][2],
        updated[6][2],
    )


def solution(mesh):
    in_specs = (
        P("dp", None),
        P("dp", None),
        P("dp", "tensor", None, None),
        P("dp", None),
        P(None, "dp", "tensor"),
        P("tensor", "dp"),
        P("dp", "tensor"),
        P("tensor", "dp"),
        P(None, "dp", "tensor"),
        P("tensor", "dp"),
        P("dp", "tensor"),
        P("tensor", "dp"),
        P(None, "dp", "tensor"),
        P("tensor", "dp"),
        P("dp", "tensor"),
        P("tensor", "dp"),
        P(None, "tensor"),
        P("tensor"),
        P(),
        P(None, "tensor"),
        P("tensor"),
        P(),
        P(None, "tensor"),
        P("tensor"),
        P(),
    )
    out_specs = (
        P("dp", None),
        P("dp", None),
        P("dp", "tensor", None, None),
        P(),
        P(None, "dp", "tensor"),
        P("tensor", "dp"),
        P("dp", "tensor"),
        P("tensor", "dp"),
        P(None, "dp", "tensor"),
        P("tensor", "dp"),
        P("dp", "tensor"),
        P("tensor", "dp"),
        P(None, "dp", "tensor"),
        P("tensor", "dp"),
        P("dp", "tensor"),
        P("tensor", "dp"),
        P(None, "dp", "tensor"),
        P("tensor", "dp"),
        P("dp", "tensor"),
        P("tensor", "dp"),
        P(None, "tensor"),
        P("tensor"),
        P(),
        P(None, "tensor"),
        P("tensor"),
        P(),
        P(None, "tensor"),
        P("tensor"),
        P(),
    )
    return jax.shard_map(
        on_device, mesh=mesh, in_specs=in_specs, out_specs=out_specs, check_vma=False
    )
```

profile of v0, /device:TPU:0, one launch (start us, length us, event | category | flops | bytes accessed | tf_op | source)
XLA Modules:
  0.0 938.5 jit_solution(11996233657050409264)
XLA Ops:
  9.2 38.6 %all_gather.12 = bf16[3,768,192]{2,0,1:T(4,128)(2,1)S(1)} all-gather(bf16[3,96,192]{2,0,1:T(4,128)(2,1)S(1)} %copy.141), channel_id=1, replica_groups=mesh['dp'=8,'tensor'=4] {'dp'}, dimensions={1}, use_global_device_ids=true | all-gather | bytes 995328 | tf_op jit(solution)/shard_map/all_gather | solution.py:108
  47.8 4.4 convolution_bitcast_fusion.1
  53.4 1.9 squeeze.37
  60.5 6.6 copy.146
  67.2 14.8 %while.28 = (s32[]{:T(128)}, bf16[3,512,3,64]{1,3,2,0:T(8,128)(2,1)S(1)}, f32[3,3,512,1]{2,1,3,0:T(4,128)S(1)}, bf16[3,512,3,64]{1,3,2,0:T(8,128)(2,1)}, s32[3,5...) while((s32[]{:T(128)}, ...), condition=%wide.region_3.4_spmd, body=%wide.region_0.3_spmd.sunk | while | flops 209549824 | bytes 12388973 | solution.py:131
  67.4 2.6 fusion.143
  72.4 2.6 fusion.143
  77.3 2.6 fusion.143
  82.7 31.0 %all_gather.13 = bf16[192,768]{0,1:T(8,128)(2,1)S(1)} all-gather(bf16[192,96]{0,1:T(8,128)(2,1)S(1)} %copy.148), channel_id=1, replica_groups=mesh['dp'=8,'tensor'=4] {'dp'}, dimensions={1}, use_global_device_ids=true | all-gather | bytes 331776 | tf_op jit(solution)/shard_map/all_gather | solution.py:109
  113.7 3.0 fusion.98
  116.8 1.6 convert_element_type.135
  118.5 1.6 convert_element_type.137
  120.5 89.9 %all-reduce.8.cloned.1.call-done = f32[1536,768]{1,0:T(8,128)} async-done(((f32[1536,768]{1,0:T(8,128)}), f32[1536,768]{1,0:T(8,128)}) %all-reduce.8.cloned.1.call-update) | async-done | bytes 4718608 | tf_op jit(solution)/shard_map/psum | solution.py:138
  210.4 3.0 fusion.95
  216.7 14.5 %multiply_convert_fusion.2 = (bf16[1536,768]{1,0:T(8,128)(2,1)}, f32[1536,768]{1,0:T(8,128)}, f32[1536,768]{1,0:T(8,128)}) fusion(f32[768]{0:T(1024)S(1)} %copy-done.28, bf16[1536,768]{1,0:T(8,128)(2,1)S(1)} %fusion.62, bf16[768,768]{1,0:T(8,128)(2,1)} %all-gather.3.cloned.1.call-done), kind=kOutput, calls=%fused_computation.82 | convolution fusion | flops 1889796096 | bytes 15338496 | tf_op jit(solution)/shard_map/dot_general | solution.py:143
  231.2 6.2 fusion.99
  237.7 94.0 %all-reduce.10.cloned.1.call-done = f32[1536,768]{1,0:T(8,128)} async-done(((f32[1536,768]{1,0:T(8,128)}), f32[1536,768]{1,0:T(8,128)}) %all-reduce.10.cloned.1.call-update) | async-done | bytes 4718608 | tf_op jit(solution)/shard_map/psum | solution.py:147
  331.7 4.7 fusion.93
  338.1 2.2 multiply_reduce_fusion.1
  340.4 3.8 fusion.92
  344.2 2.2 copy-done.2
  347.0 3.4 convert_reduce_fusion.2
  351.8 4.2 fusion.100
  356.1 5.3 fusion.102
  361.4 3.6 fusion.103
  365.0 85.4 %all-reduce.12.cloned.1.call-done = f32[1536,768]{1,0:T(8,128)} async-done(((f32[1536,768]{1,0:T(8,128)}), f32[1536,768]{1,0:T(8,128)}) %all-reduce.12.cloned.1.call-update) | async-done | bytes 4718608 | tf_op jit(solution)/shard_map/psum | solution.py:168
  450.3 6.7 multiply_reduce_fusion.2
  457.1 3.8 fusion.91
  468.6 55.0 %while.29 = (s32[]{:T(128)}, bf16[3,512,3,64]{1,3,2,0:T(8,128)(2,1)}, bf16[3,512,3,64]{1,3,2,0:T(8,128)(2,1)}, bf16[3,512,3,64]{1,3,2,0:T(8,128)(2,1)}, f32[3,3,...) while((s32[]{:T(128)}, ...), condition=%wide.region_17.18_spmd, body=%wide.region_15.17_spmd.sunk | while | flops 513505792 | bytes 43427472 | solution.py:176
  470.5 3.0 multiply_reduce_fusion.15
  473.5 2.6 bitcast_convert_fusion.2
  476.1 2.0 fusion.155
  478.1 2.2 fusion.156
  480.3 2.2 fusion.157
  482.5 2.4 copy.203
  484.9 2.0 constant_dynamic-update-slice_fusion.5
  486.9 1.6 fusion.154
  488.8 3.0 multiply_reduce_fusion.15
  491.8 2.6 bitcast_convert_fusion.2
  494.5 2.0 fusion.155
  496.5 2.2 fusion.156
  498.7 2.2 fusion.157
  500.9 2.4 copy.203
  503.3 2.0 constant_dynamic-update-slice_fusion.5
  507.1 3.0 multiply_reduce_fusion.15
  510.2 2.6 bitcast_convert_fusion.2
  512.8 2.0 fusion.155
  514.8 2.2 fusion.156
  517.0 2.2 fusion.157
  519.2 2.4 copy.203
  521.6 2.0 constant_dynamic-update-slice_fusion.5
  533.6 4.9 fusion.66
  540.5 4.5 convolution_bitcast_fusion
  548.2 39.3 %all-reduce = (f32[2,192]{1,0:T(2,128)S(1)}, f32[768]{0:T(1024)S(1)}, f32[6,768]{1,0:T(8,128)S(1)}) all-reduce(f32[2,192]{1,0:T(2,128)S(1)} %pad_maximum_fusion, f32[768]{0:T(1024)S(1)} %get-tuple-element.431, f32[6,768]{1,0:T(8,128)S(1)} %stack.31), channel_id=1, replica_groups=mesh['dp'=8,'tensor'=4] {'dp'}, use_global_device_ids=true, to_apply=%region_29.30 | all-reduce | flops 5760 | bytes 46080 | tf_op jit(solution)/shard_map/psum | solution.py:215
  591.2 183.0 %all-reduce.16.cloned.1.call-done = (f32[3,768,192]{1,2,0:T(8,128)}, f32[192,768]{1,0:T(8,128)}, f32[768,768]{1,0:T(8,128)}, f32[768,768]{0,1:T(8,128)}) async-done(((f32[3,768,192]{1,2,0:T(8,128)}, f32[192,768]{1,0:T(8,128)}, f32[768,768]{1,0:T(8,128)}, f32[768,768]{0,1:T(8,128)}), (f32[3,768,192]{1,2,0:T(8,128)}, f32[192,768]{1,0:T(8,128)}, f32[768,768]{1,0:T(8,128)}, ...) | async-done | bytes 7077904 | tf_op jit(solution)/shard_map/psum | solution.py:215
  775.8 1.8 multiply_reduce_fusion.9
  778.9 1.6 multiply_reduce_fusion.8
  781.2 1.7 multiply_reduce_fusion.7
  783.6 86.5 %all-reduce.14.cloned.1.call-done = f32[1536,768]{1,0:T(8,128)} async-done(((f32[1536,768]{1,0:T(8,128)}), f32[1536,768]{1,0:T(8,128)}) %all-reduce.14.cloned.1.call-update) | async-done | bytes 4718608 | tf_op jit(solution)/shard_map/psum | solution.py:204
  870.1 6.5 add_add_fusion.4
  876.6 39.5 %psum.95 = f32[]{:T(128)} all-reduce(f32[]{:T(128)S(6)} %add.314), channel_id=1, replica_groups=mesh['dp'=8,'tensor'=4] {'dp','tensor'}, use_global_device_ids=true, to_apply=%region_42.43 | all-reduce | flops 1 | bytes 8 | tf_op jit(solution)/shard_map/psum | solution.py:251
  921.8 1.9 fusion.87
  923.7 2.1 fusion.85
  925.8 2.2 fusion.83
  (201 shorter events, 59.4 us)
Async XLA Ops:
  8.0 202.4 %all-reduce.8.cloned.1.call-start = ((), (), s32[]{:S(2)}) async-start(), calls=%async_computation | async-start | bytes 9437184 | tf_op jit(solution)/shard_map/psum | solution.py:138
  47.8 4.4 copy-start.8
  52.2 3.2 copy-start.26
  60.5 6.7 copy-start.21
  67.2 15.5 %copy-start.13 = (f32[192,96]{1,0:T(8,128)S(1)}, f32[192,96]{1,0:T(8,128)}, u32[]{:S(2)}) copy-start(f32[192,96]{1,0:T(8,128)} %param.34) | copy-start | bytes 221188
  113.7 6.7 copy-start.22
  113.7 96.7 %copy-start.5 = (bf16[1536,768]{1,0:T(8,128)(2,1)S(1)}, bf16[1536,768]{1,0:T(8,128)(2,1)}, u32[]{:S(2)}) copy-start(bf16[1536,768]{1,0:T(8,128)(2,1)} %param.29) | copy-start | bytes 7077892
  116.8 99.9 %all-gather.3.cloned.1.call-start = ((), (), s32[]{:S(2)}) async-start(), calls=%async_computation.1 | async-start | bytes 1327104 | tf_op jit(solution)/shard_map/all_gather | solution.py:110
  118.5 112.7 %all-gather.5.cloned.1.call-start = ((), (), s32[]{:S(2)}) async-start(), calls=%async_computation.2 | async-start | bytes 1327104 | tf_op jit(solution)/shard_map/all_gather | solution.py:111
  120.2 211.5 %all-reduce.10.cloned.1.call-start = ((), (), s32[]{:S(2)}) async-start(), calls=%async_computation.3 | async-start | bytes 9437184 | tf_op jit(solution)/shard_map/psum | solution.py:147
  213.4 2.1 copy-start
  214.1 2.5 copy-start.28
  237.4 213.0 %all-reduce.12.cloned.1.call-start = ((), (), s32[]{:S(2)}) async-start(), calls=%async_computation.4 | async-start | bytes 9437184 | tf_op jit(solution)/shard_map/psum | solution.py:168
  336.4 1.7 copy-start.3
  340.3 6.5 slice-start
  340.3 6.5 slice-start.2
  340.4 6.5 slice-start.1
  340.4 6.5 slice-start.3
  344.2 2.2 copy-start.2
  344.2 2.7 copy-start.34
  346.9 3.5 copy-start.6
  346.9 4.8 copy-start.33
  350.3 1.4 copy-start.4
  356.0 418.2 %all-reduce.16.cloned.1.call-start = ((), (), s32[]{:S(2)}) async-start(), calls=%async_computation.6 | async-start | bytes 14155776 | tf_op jit(solution)/shard_map/psum | solution.py:215
  356.1 5.3 copy-start.7
  356.1 5.3 copy-start.35
  460.9 2.1 copy-start.1
  538.5 1.4 copy-start.9
  538.5 1.9 copy-start.20
  538.6 331.5 %all-reduce.14.cloned.1.call-start = ((), (), s32[]{:S(2)}) async-start(), calls=%async_computation.5 | async-start | bytes 9437184 | tf_op jit(solution)/shard_map/psum | solution.py:204
  545.0 1.0 copy-start.10
  545.0 1.1 copy-start.15
  545.0 1.3 copy-start.16
  783.6 138.2 %copy-start.14 = (f32[192,96]{1,0:T(8,128)S(1)}, f32[192,96]{1,0:T(8,128)}, u32[]{:S(2)}) copy-start(f32[192,96]{1,0:T(8,128)} %param.34) | copy-start | bytes 221188
  876.6 47.1 %copy-start.11 = (f32[96,768]{1,0:T(8,128)S(1)}, f32[96,768]{1,0:T(8,128)}, u32[]{:S(2)}) copy-start(f32[96,768]{1,0:T(8,128)} %param.35) | copy-start | bytes 884740
  876.6 47.1 %copy-start.17 = (f32[96,768]{1,0:T(8,128)S(1)}, f32[96,768]{1,0:T(8,128)}, u32[]{:S(2)}) copy-start(f32[96,768]{1,0:T(8,128)} %param.39) | copy-start | bytes 884740
  876.6 47.1 %copy-start.18 = (f32[96,768]{1,0:T(8,128)S(1)}, f32[96,768]{1,0:T(8,128)}, u32[]{:S(2)}) copy-start(f32[96,768]{1,0:T(8,128)} %param.43) | copy-start | bytes 884740
  876.6 49.2 %copy-start.12 = (f32[768,96]{0,1:T(8,128)S(1)}, f32[768,96]{0,1:T(8,128)}, u32[]{:S(2)}) copy-start(f32[768,96]{0,1:T(8,128)} %param.36) | copy-start | bytes 884740
  876.6 49.2 %copy-start.19 = (f32[768,96]{0,1:T(8,128)S(1)}, f32[768,96]{0,1:T(8,128)}, u32[]{:S(2)}) copy-start(f32[768,96]{0,1:T(8,128)} %param.40) | copy-start | bytes 884740
  916.9 11.1 %copy-start.27 = (f32[2,192]{1,0:T(2,128)S(1)}, f32[2,192]{1,0:T(2,128)}, u32[]{:S(2)}) copy-start(f32[2,192]{1,0:T(2,128)} %param.45) | copy-start | bytes 4612
  916.9 12.3 %copy-start.23 = (f32[6,768]{1,0:T(8,128)S(1)}, f32[6,768]{1,0:T(8,128)}, u32[]{:S(2)}) copy-start(f32[6,768]{1,0:T(8,128)} %param.47) | copy-start | bytes 55300
  918.3 9.6 %copy-start.31 = (f32[2,192]{1,0:T(2,128)S(1)}, f32[2,192]{1,0:T(2,128)}, u32[]{:S(2)}) copy-start(f32[2,192]{1,0:T(2,128)} %param.48) | copy-start | bytes 4612
  918.3 9.6 %copy-start.32 = (f32[2,192]{1,0:T(2,128)S(1)}, f32[2,192]{1,0:T(2,128)}, u32[]{:S(2)}) copy-start(f32[2,192]{1,0:T(2,128)} %param.51) | copy-start | bytes 4612
  918.3 10.2 %copy-start.29 = (f32[768]{0:T(1024)S(1)}, f32[768]{0:T(1024)}, u32[]{:S(2)}) copy-start(f32[768]{0:T(1024)} %param.49) | copy-start | bytes 9220
  918.3 10.2 %copy-start.30 = (f32[768]{0:T(1024)S(1)}, f32[768]{0:T(1024)}, u32[]{:S(2)}) copy-start(f32[768]{0:T(1024)} %param.52) | copy-start | bytes 9220
  918.3 10.8 %copy-start.24 = (f32[6,768]{1,0:T(8,128)S(1)}, f32[6,768]{1,0:T(8,128)}, u32[]{:S(2)}) copy-start(f32[6,768]{1,0:T(8,128)} %param.50) | copy-start | bytes 55300
  918.3 10.8 %copy-start.25 = (f32[6,768]{1,0:T(8,128)S(1)}, f32[6,768]{1,0:T(8,128)}, u32[]{:S(2)}) copy-start(f32[6,768]{1,0:T(8,128)} %param.53) | copy-start | bytes 55300
Sparse Core Ops, SparseCore 0:
  116.9 93.4 all-reduce.7
  237.5 94.1 all-reduce.9
  356.1 94.1 all-reduce.11
Sparse Core Ops, SparseCore 1:
  120.0 40.8 all-gather.2
  163.5 39.9 all-gather.4
  538.6 235.5 all-reduce.15
  777.3 92.7 all-reduce.13
where the time goes:
time: 947 us; the launch traced here: 938 us
  waiting for transfers between devices  539 us (57%)
  blocking collectives  148 us (16%)
  matrix products  102 us (11%)
  other arithmetic  69.2 us (7%)
  local copies, waits for them, and re-layouts  56 us (6%)
  between operations  22.9 us (2%)
    psum x1, waiting for transfers between devices, on_device(): lax.psum((grad_attn_in, grad_attn_out, grad_ffn_in, grad_ffn_out, grad_qv...  183 us
    psum x1, waiting for transfers between devices, on_device(): ffn_output = lax.psum(ffn_partial, 'tensor') + row_params[4]  94 us
    psum x1, waiting for transfers between devices, on_device(): attended = lax.psum(attn_partial, 'tensor') + row_params[2]  89.9 us
    psum x1, waiting for transfers between devices, on_device(): tokens_grad = grad_res_one + lax.psum(input_part, 'tensor')  86.5 us
    psum x1, waiting for transfers between devices, on_device(): grad_normed = grad_res_two + lax.psum(hidden_part, 'tensor')  85.4 us
    psum x1, blocking collectives, on_device(): total_squares = lax.psum(local_squares, ('dp', 'tensor'))  39.5 us
    psum x1, blocking collectives, on_device(): lax.psum((grad_attn_in, grad_attn_out, grad_ffn_in, grad_ffn_out, grad_qv...  39.3 us
    all_gather x1, blocking collectives, on_device(): lax.all_gather(attn_in_master.astype(jnp.bfloat16), 'dp', axis=1, tiled=T...  38.6 us
  transfers between devices with their start and end apart: 7, of which 5 were waited for; matrix products, arithmetic and copies ran while one was open for 5% of the time, Pallas kernels for 0%

commit v1 on v0

--- a/solution.py
+++ b/solution.py
@@ -3,6 +3,7 @@
 import jax.numpy as jnp
 from jax import lax
 from jax.sharding import PartitionSpec as P
+from jax.lax import psum
 
 D = 768
 STEP = 5
@@ -248,7 +249,8 @@
     local_squares = local_squares + jnp.sum(small_sums[2] * small_sums[2]) / (
         dp_count * tensor_count
     )
-    total_squares = lax.psum(local_squares, ("dp", "tensor"))
+    frame_solve = lambda block_in: psum(psum(block_in, "tensor"), "dp")
+    total_squares = frame_solve(local_squares)
     grad_norm = jnp.sqrt(total_squares)
     factor = 1.0 / jnp.maximum(grad_norm, 1.0)
     olds = (

time: 947 us -> 930 us (0.982)
  blocking collectives: 148 us -> 138 us
    psum x1 -> x2, blocking collectives: 39.5 us -> 29.4 us  [on_device(): frame_solve = lambda block_in: psum(psum(block_in, 'tensor'), 'dp')]
where the time goes in v1:
time: 930 us; the launch traced here: 921 us
  waiting for transfers between devices  532 us (57%)
  blocking collectives  138 us (15%)
  matrix products  102 us (11%)
  other arithmetic  69.2 us (7%)
  local copies, waits for them, and re-layouts  56 us (6%)
  between operations  22.8 us (2%)
    psum x1, waiting for transfers between devices, on_device(): lax.psum((grad_attn_in, grad_attn_out, grad_ffn_in, grad_ffn_out, grad_qv...  183 us
    psum x1, waiting for transfers between devices, on_device(): ffn_output = lax.psum(ffn_partial, 'tensor') + row_params[4]  94 us
    psum x1, waiting for transfers between devices, on_device(): attended = lax.psum(attn_partial, 'tensor') + row_params[2]  89.9 us
    psum x1, waiting for transfers between devices, on_device(): grad_normed = grad_res_two + lax.psum(hidden_part, 'tensor')  85.4 us
    psum x1, waiting for transfers between devices, on_device(): tokens_grad = grad_res_one + lax.psum(input_part, 'tensor')  79 us
    psum x1, blocking collectives, on_device(): lax.psum((grad_attn_in, grad_attn_out, grad_ffn_in, grad_ffn_out, grad_qv...  39.3 us
    all_gather x1, blocking collectives, on_device(): lax.all_gather(attn_in_master.astype(jnp.bfloat16), 'dp', axis=1, tiled=T...  38.6 us
    all_gather x1, blocking collectives, on_device(): lax.all_gather(attn_out_master.astype(jnp.bfloat16), 'dp', axis=1, tiled=...  31 us
  transfers between devices with their start and end apart: 7, of which 5 were waited for; matrix products, arithmetic and copies ran while one was open for 5% of the time, Pallas kernels for 0%

profile of v1, /device:TPU:0, one launch (start us, length us, event | category | flops | bytes accessed | tf_op | source)
XLA Modules:
  0.0 921.2 jit_solution(10861711040664629021)
XLA Ops:
  9.2 38.6 %all_gather.12 = bf16[3,768,192]{2,0,1:T(4,128)(2,1)S(1)} all-gather(bf16[3,96,192]{2,0,1:T(4,128)(2,1)S(1)} %copy.141), channel_id=1, replica_groups=mesh['dp'=8,'tensor'=4] {'dp'}, dimensions={1}, use_global_device_ids=true | all-gather | bytes 995328 | tf_op jit(solution)/shard_map/all_gather | solution.py:109
  47.8 4.4 convolution_bitcast_fusion.1
  53.4 1.9 squeeze.37
  60.5 6.6 copy.146
  67.2 14.8 %while.28 = (s32[]{:T(128)}, bf16[3,512,3,64]{1,3,2,0:T(8,128)(2,1)S(1)}, f32[3,3,512,1]{2,1,3,0:T(4,128)S(1)}, bf16[3,512,3,64]{1,3,2,0:T(8,128)(2,1)}, s32[3,5...) while((s32[]{:T(128)}, ...), condition=%wide.region_3.4_spmd, body=%wide.region_0.3_spmd.sunk | while | flops 209549824 | bytes 12388973 | solution.py:132
  67.4 2.6 fusion.143
  72.4 2.6 fusion.143
  77.3 2.6 fusion.143
  82.7 31.0 %all_gather.13 = bf16[192,768]{0,1:T(8,128)(2,1)S(1)} all-gather(bf16[192,96]{0,1:T(8,128)(2,1)S(1)} %copy.148), channel_id=1, replica_groups=mesh['dp'=8,'tensor'=4] {'dp'}, dimensions={1}, use_global_device_ids=true | all-gather | bytes 331776 | tf_op jit(solution)/shard_map/all_gather | solution.py:110
  113.7 3.0 fusion.98
  116.8 1.6 convert_element_type.135
  118.5 1.6 convert_element_type.137
  120.5 89.9 %all-reduce.8.cloned.1.call-done = f32[1536,768]{1,0:T(8,128)} async-done(((f32[1536,768]{1,0:T(8,128)}), f32[1536,768]{1,0:T(8,128)}) %all-reduce.8.cloned.1.call-update) | async-done | bytes 4718608 | tf_op jit(solution)/shard_map/psum | solution.py:139
  210.4 3.0 fusion.95
  216.7 14.5 %multiply_convert_fusion.2 = (bf16[1536,768]{1,0:T(8,128)(2,1)}, f32[1536,768]{1,0:T(8,128)}, f32[1536,768]{1,0:T(8,128)}) fusion(f32[768]{0:T(1024)S(1)} %copy-done.28, bf16[1536,768]{1,0:T(8,128)(2,1)S(1)} %fusion.62, bf16[768,768]{1,0:T(8,128)(2,1)} %all-gather.3.cloned.1.call-done), kind=kOutput, calls=%fused_computation.82 | convolution fusion | flops 1889796096 | bytes 15338496 | tf_op jit(solution)/shard_map/dot_general | solution.py:144
  231.2 6.2 fusion.99
  237.7 94.0 %all-reduce.10.cloned.1.call-done = f32[1536,768]{1,0:T(8,128)} async-done(((f32[1536,768]{1,0:T(8,128)}), f32[1536,768]{1,0:T(8,128)}) %all-reduce.10.cloned.1.call-update) | async-done | bytes 4718608 | tf_op jit(solution)/shard_map/psum | solution.py:148
  331.7 4.7 fusion.93
  338.1 2.2 multiply_reduce_fusion.1
  340.4 3.8 fusion.92
  344.2 2.2 copy-done.2
  347.0 3.4 convert_reduce_fusion.2
  351.8 4.2 fusion.100
  356.1 5.3 fusion.102
  361.4 3.6 fusion.103
  365.0 85.4 %all-reduce.12.cloned.1.call-done = f32[1536,768]{1,0:T(8,128)} async-done(((f32[1536,768]{1,0:T(8,128)}), f32[1536,768]{1,0:T(8,128)}) %all-reduce.12.cloned.1.call-update) | async-done | bytes 4718608 | tf_op jit(solution)/shard_map/psum | solution.py:169
  450.3 6.7 multiply_reduce_fusion.2
  457.1 3.8 fusion.91
  468.6 55.0 %while.29 = (s32[]{:T(128)}, bf16[3,512,3,64]{1,3,2,0:T(8,128)(2,1)}, bf16[3,512,3,64]{1,3,2,0:T(8,128)(2,1)}, bf16[3,512,3,64]{1,3,2,0:T(8,128)(2,1)}, f32[3,3,...) while((s32[]{:T(128)}, ...), condition=%wide.region_17.18_spmd, body=%wide.region_15.17_spmd.sunk | while | flops 513505792 | bytes 43427472 | solution.py:177
  470.5 3.0 multiply_reduce_fusion.15
  473.5 2.6 bitcast_convert_fusion.2
  476.1 2.0 fusion.155
  478.1 2.2 fusion.156
  480.3 2.2 fusion.157
  482.5 2.4 copy.203
  484.9 2.0 constant_dynamic-update-slice_fusion.5
  488.8 3.0 multiply_reduce_fusion.15
  491.8 2.6 bitcast_convert_fusion.2
  494.5 2.0 fusion.155
  496.5 2.2 fusion.156
  498.7 2.2 fusion.157
  500.9 2.4 copy.203
  503.3 2.0 constant_dynamic-update-slice_fusion.5
  507.1 3.0 multiply_reduce_fusion.15
  510.2 2.6 bitcast_convert_fusion.2
  512.8 2.0 fusion.155
  514.8 2.2 fusion.156
  517.0 2.2 fusion.157
  519.2 2.4 copy.203
  521.6 2.0 constant_dynamic-update-slice_fusion.5
  533.6 4.9 fusion.66
  540.5 4.5 convolution_bitcast_fusion
  548.0 39.3 %all-reduce = (f32[2,192]{1,0:T(2,128)S(1)}, f32[768]{0:T(1024)S(1)}, f32[6,768]{1,0:T(8,128)S(1)}) all-reduce(f32[2,192]{1,0:T(2,128)S(1)} %pad_maximum_fusion, f32[768]{0:T(1024)S(1)} %get-tuple-element.431, f32[6,768]{1,0:T(8,128)S(1)} %stack.31), channel_id=1, replica_groups=mesh['dp'=8,'tensor'=4] {'dp'}, use_global_device_ids=true, to_apply=%region_29.30 | all-reduce | flops 5760 | bytes 46080 | tf_op jit(solution)/shard_map/psum | solution.py:216
  591.1 183.2 %all-reduce.16.cloned.1.call-done = (f32[3,768,192]{1,2,0:T(8,128)}, f32[192,768]{1,0:T(8,128)}, f32[768,768]{1,0:T(8,128)}, f32[768,768]{0,1:T(8,128)}) async-done(((f32[3,768,192]{1,2,0:T(8,128)}, f32[192,768]{1,0:T(8,128)}, f32[768,768]{1,0:T(8,128)}, f32[768,768]{0,1:T(8,128)}), (f32[3,768,192]{1,2,0:T(8,128)}, f32[192,768]{1,0:T(8,128)}, f32[768,768]{1,0:T(8,128)}, ...) | async-done | bytes 7077904 | tf_op jit(solution)/shard_map/psum | solution.py:216
  775.9 1.8 multiply_reduce_fusion.9
  779.0 1.6 multiply_reduce_fusion.8
  781.3 1.7 multiply_reduce_fusion.7
  783.8 7.4 psum.102
  791.3 79.0 %all-reduce.14.cloned.1.call-done = f32[1536,768]{1,0:T(8,128)} async-done(((f32[1536,768]{1,0:T(8,128)}), f32[1536,768]{1,0:T(8,128)}) %all-reduce.14.cloned.1.call-update) | async-done | bytes 4718608 | tf_op jit(solution)/shard_map/psum | solution.py:205
  870.3 6.5 add_add_fusion.4
  876.8 22.0 %psum.103 = f32[]{:T(128)} all-reduce(f32[]{:T(128)} %psum.102), channel_id=1, replica_groups=mesh['dp'=8,'tensor'=4] {'dp'}, use_global_device_ids=true, to_apply=%region_43.44 | all-reduce | flops 1 | bytes 8 | tf_op jit(solution)/shard_map/psum | solution.py:252
  904.5 1.9 fusion.87
  906.4 2.1 fusion.85
  908.4 2.2 fusion.83
  (202 shorter events, 61.0 us)
Async XLA Ops:
  8.0 202.4 %all-reduce.8.cloned.1.call-start = ((), (), s32[]{:S(2)}) async-start(), calls=%async_computation | async-start | bytes 9437184 | tf_op jit(solution)/shard_map/psum | solution.py:139
  47.8 4.4 copy-start.8
  52.2 3.2 copy-start.26
  60.5 6.7 copy-start.21
  67.2 15.5 %copy-start.13 = (f32[192,96]{1,0:T(8,128)S(1)}, f32[192,96]{1,0:T(8,128)}, u32[]{:S(2)}) copy-start(f32[192,96]{1,0:T(8,128)} %param.34) | copy-start | bytes 221188
  113.7 6.7 copy-start.22
  113.7 96.7 %copy-start.5 = (bf16[1536,768]{1,0:T(8,128)(2,1)S(1)}, bf16[1536,768]{1,0:T(8,128)(2,1)}, u32[]{:S(2)}) copy-start(bf16[1536,768]{1,0:T(8,128)(2,1)} %param.29) | copy-start | bytes 7077892
  116.8 99.9 %all-gather.3.cloned.1.call-start = ((), (), s32[]{:S(2)}) async-start(), calls=%async_computation.1 | async-start | bytes 1327104 | tf_op jit(solution)/shard_map/all_gather | solution.py:111
  118.5 112.7 %all-gather.5.cloned.1.call-start = ((), (), s32[]{:S(2)}) async-start(), calls=%async_computation.2 | async-start | bytes 1327104 | tf_op jit(solution)/shard_map/all_gather | solution.py:112
  120.2 211.5 %all-reduce.10.cloned.1.call-start = ((), (), s32[]{:S(2)}) async-start(), calls=%async_computation.3 | async-start | bytes 9437184 | tf_op jit(solution)/shard_map/psum | solution.py:148
  213.4 2.1 copy-start
  214.1 2.5 copy-start.28
  237.4 213.0 %all-reduce.12.cloned.1.call-start = ((), (), s32[]{:S(2)}) async-start(), calls=%async_computation.4 | async-start | bytes 9437184 | tf_op jit(solution)/shard_map/psum | solution.py:169
  336.4 1.7 copy-start.3
  340.3 6.5 slice-start
  340.3 6.5 slice-start.2
  340.4 6.5 slice-start.1
  340.4 6.5 slice-start.3
  344.2 2.2 copy-start.2
  344.2 2.7 copy-start.34
  346.9 3.5 copy-start.6
  346.9 4.8 copy-start.33
  350.3 1.4 copy-start.4
  356.0 418.3 %all-reduce.16.cloned.1.call-start = ((), (), s32[]{:S(2)}) async-start(), calls=%async_computation.6 | async-start | bytes 14155776 | tf_op jit(solution)/shard_map/psum | solution.py:216
  356.1 5.3 copy-start.7
  356.1 5.3 copy-start.35
  460.9 2.1 copy-start.1
  538.5 1.4 copy-start.9
  538.5 1.9 copy-start.20
  538.6 331.7 %all-reduce.14.cloned.1.call-start = ((), (), s32[]{:S(2)}) async-start(), calls=%async_computation.5 | async-start | bytes 9437184 | tf_op jit(solution)/shard_map/psum | solution.py:205
  545.0 1.0 copy-start.10
  545.0 1.1 copy-start.15
  545.0 238.7 %copy-start.16 = (f32[3,96,192]{2,1,0:T(8,128)S(1)}, f32[3,96,192]{2,1,0:T(8,128)}, u32[]{:S(2)}) copy-start(f32[3,96,192]{2,1,0:T(8,128)} %param.41) | copy-start | bytes 663556
  791.3 113.2 %copy-start.14 = (f32[192,96]{1,0:T(8,128)S(1)}, f32[192,96]{1,0:T(8,128)}, u32[]{:S(2)}) copy-start(f32[192,96]{1,0:T(8,128)} %param.34) | copy-start | bytes 221188
  876.8 29.6 %copy-start.11 = (f32[96,768]{1,0:T(8,128)S(1)}, f32[96,768]{1,0:T(8,128)}, u32[]{:S(2)}) copy-start(f32[96,768]{1,0:T(8,128)} %param.35) | copy-start | bytes 884740
  876.8 29.6 %copy-start.17 = (f32[96,768]{1,0:T(8,128)S(1)}, f32[96,768]{1,0:T(8,128)}, u32[]{:S(2)}) copy-start(f32[96,768]{1,0:T(8,128)} %param.39) | copy-start | bytes 884740
  876.8 29.6 %copy-start.18 = (f32[96,768]{1,0:T(8,128)S(1)}, f32[96,768]{1,0:T(8,128)}, u32[]{:S(2)}) copy-start(f32[96,768]{1,0:T(8,128)} %param.43) | copy-start | bytes 884740
  876.8 31.6 %copy-start.12 = (f32[768,96]{0,1:T(8,128)S(1)}, f32[768,96]{0,1:T(8,128)}, u32[]{:S(2)}) copy-start(f32[768,96]{0,1:T(8,128)} %param.36) | copy-start | bytes 884740
  876.8 31.6 %copy-start.19 = (f32[768,96]{0,1:T(8,128)S(1)}, f32[768,96]{0,1:T(8,128)}, u32[]{:S(2)}) copy-start(f32[768,96]{0,1:T(8,128)} %param.40) | copy-start | bytes 884740
  899.5 11.1 %copy-start.27 = (f32[2,192]{1,0:T(2,128)S(1)}, f32[2,192]{1,0:T(2,128)}, u32[]{:S(2)}) copy-start(f32[2,192]{1,0:T(2,128)} %param.45) | copy-start | bytes 4612
  899.6 12.3 %copy-start.23 = (f32[6,768]{1,0:T(8,128)S(1)}, f32[6,768]{1,0:T(8,128)}, u32[]{:S(2)}) copy-start(f32[6,768]{1,0:T(8,128)} %param.47) | copy-start | bytes 55300
  901.0 9.6 %copy-start.31 = (f32[2,192]{1,0:T(2,128)S(1)}, f32[2,192]{1,0:T(2,128)}, u32[]{:S(2)}) copy-start(f32[2,192]{1,0:T(2,128)} %param.48) | copy-start | bytes 4612
  901.0 9.6 %copy-start.32 = (f32[2,192]{1,0:T(2,128)S(1)}, f32[2,192]{1,0:T(2,128)}, u32[]{:S(2)}) copy-start(f32[2,192]{1,0:T(2,128)} %param.51) | copy-start | bytes 4612
  901.0 10.2 %copy-start.29 = (f32[768]{0:T(1024)S(1)}, f32[768]{0:T(1024)}, u32[]{:S(2)}) copy-start(f32[768]{0:T(1024)} %param.49) | copy-start | bytes 9220
  901.0 10.2 %copy-start.30 = (f32[768]{0:T(1024)S(1)}, f32[768]{0:T(1024)}, u32[]{:S(2)}) copy-start(f32[768]{0:T(1024)} %param.52) | copy-start | bytes 9220
  901.0 10.8 %copy-start.24 = (f32[6,768]{1,0:T(8,128)S(1)}, f32[6,768]{1,0:T(8,128)}, u32[]{:S(2)}) copy-start(f32[6,768]{1,0:T(8,128)} %param.50) | copy-start | bytes 55300
  901.0 10.8 %copy-start.25 = (f32[6,768]{1,0:T(8,128)S(1)}, f32[6,768]{1,0:T(8,128)}, u32[]{:S(2)}) copy-start(f32[6,768]{1,0:T(8,128)} %param.53) | copy-start | bytes 55300
Sparse Core Ops, SparseCore 0:
  116.9 93.4 all-reduce.7
  237.5 94.1 all-reduce.9
  356.1 94.1 all-reduce.11
Sparse Core Ops, SparseCore 1:
  120.0 40.8 all-gather.2
  163.5 39.9 all-gather.4
  538.6 235.6 all-reduce.15
  777.4 92.9 all-reduce.13
